TPU v7x, 32 devices: a whole 2x2x4 slice. The times are simulated.
32 devices in a mesh: planes: 16 (over z, y, x), elem: 2 (over core).
Axes of the slice: x: 2, y: 2, z: 4, core: 2. Of those that a mesh axis runs over, the one named last changes fastest.
Arguments:
- velocity: float32 [3, 256, 20736], P(None, 'planes', 'elem'), may hold values from -6 to 6
- geometry: float32 [4, 20736], P(None, 'elem'), may hold values from -1.5 to 1.5
- element_kind: int32 [256], P('elem'), may hold values from 0 to 1
- element_scale: float32 [256], P('elem'), may hold values from 0.5 to 2
- dirichlet: int32 [2, 9, 256], P(None, None, 'elem'), may hold values 0 or 1
- schur_stiffness: float32 [2, 36, 36], replicated, may hold values from -0.2 to 8.5, as said below
- schur_mass: float32 [2, 36, 36], replicated, may hold values from -0.1 to 4.5, as said below
- lift: float32 [2, 36, 81], replicated, may hold values from -0.625 to 0.625
- recover: float32 [2, 81, 36], replicated, may hold values from -1 to 1
Outputs:
- new_velocity: float32 [3, 256, 20736], P(None, 'planes', 'elem')
Inputs may be any that keep to these rules, and one draw needn't show every extreme that they name: `schur_stiffness`: each of the two matrices is symmetric and positive definite. `schur_mass`: each of the two matrices is symmetric and positive definite.
All inputs are finite; a program needn't handle non-finite values. No bound on the sum of `dirichlet` on one device may be relied on, other than what follows from the above.
Results may differ from a plain program's by a relative error of at most 0.0001.
Values sent between devices are 32-bit elements; how exact they have to be, the bound alone decides.
A program may use at most 128 MiB of HBM per device.

v0:
```python
import math

import jax
import jax.numpy as jnp
import numpy as np
from jax import lax
from jax.experimental import pallas as pl
from jax.experimental.pallas import tpu as pltpu
from jax.sharding import PartitionSpec as P

PLANES = 256
QUAD = 9
COLUMN_ELEMS = 32
CG_STEPS = 4


HIGHEST = lax.Precision.HIGHEST
SIGMA_COEF = 1.0
BETA_COEF = 0.01
STEP_DT = 0.002


def passed_along(value, axis, steps):
    count = lax.axis_size(axis)
    leading, last = (max(0, -steps), min(count, count - steps))
    return lax.ppermute(value, axis, [(source, source + steps) for source in range(leading, last)])


def gauss_derivative(points):
    nodes = -np.cos(np.pi * (2 * np.arange(points) + 1) / (2 * points))
    ident = np.eye(points)
    diffs = nodes[:, None] - nodes[None, :] + ident
    weights = 1.0 / np.prod(diffs, axis=1)
    matrix = weights[None, :] / weights[:, None] / diffs
    matrix = matrix * (1.0 - ident)
    return matrix - ident * matrix.sum(axis=1)[:, None]


def kron_tables():
    deriv = gauss_derivative(QUAD)
    identity = np.eye(QUAD)
    return (
        jnp.asarray(np.kron(deriv, identity), jnp.float32),
        jnp.asarray(np.kron(identity, deriv), jnp.float32),
    )


def fourier_tables(planes):
    zeta = jnp.arange(planes, dtype=jnp.int32)
    rows = jnp.arange(planes, dtype=jnp.int32)
    waves = (rows + 1) // 2
    phase = waves[None, :] * zeta[:, None] % planes
    angle = 2.0 * math.pi / planes * phase.astype(jnp.float32)
    cosine = jnp.cos(angle)
    sine = jnp.sin(angle)
    odd = (rows % 2 == 1)[None, :]
    first = (rows == 0)[None, :]
    last = (rows == planes - 1)[None, :]
    synth = jnp.where(first, 1.0, jnp.where(odd, cosine, sine))
    rate = BETA_COEF * waves.astype(jnp.float32)[None, :]
    slope = jnp.where(first | last, 0.0, jnp.where(odd, -rate * sine, rate * cosine))
    weight = jnp.where((rows == 0) | (rows == planes - 1), 1.0 / planes, 2.0 / planes).astype(
        jnp.float32
    )
    analysis = synth.T * weight[:, None]
    return (synth, slope, analysis)


def inner(first_pair, second_pair):
    return jnp.sum(first_pair[0] * second_pair[0], axis=(0, 2)) + jnp.sum(
        first_pair[1] * second_pair[1], axis=(0, 2)
    )


def global_total(first_pair, second_pair):
    return lax.psum(inner(first_pair, second_pair), "elem")


def global_squares(pair):
    return lax.psum(inner(pair, pair), "elem")


def assemble(outputs, incoming, free):
    left = outputs[:QUAD]
    right = outputs[QUAD : 2 * QUAD]
    bottom = outputs[2 * QUAD : 3 * QUAD]
    top = outputs[3 * QUAD :]
    vertical = left + jnp.concatenate([incoming, right[:, :, :-COLUMN_ELEMS]], axis=2)
    grid = top.reshape(top.shape[0], top.shape[1], -1, COLUMN_ELEMS)
    shifted = jnp.concatenate([jnp.zeros_like(grid[..., :1]), grid[..., :-1]], axis=3).reshape(
        bottom.shape
    )
    horizontal = bottom + shifted
    return (vertical * free[0], horizontal * free[1])


def plain_device(
    velocity,
    geometry,
    element_kind,
    element_scale,
    dirichlet,
    schur_stiffness,
    schur_mass,
    lift,
    recover,
):
    first, second = kron_tables()
    synth, slope, analysis = fourier_tables(PLANES)
    local_rows = velocity.shape[1]
    node_count = velocity.shape[2]
    share = node_count // lax.axis_size("planes")
    geo_part = lax.dynamic_slice_in_dim(geometry, lax.axis_index("planes") * share, share, 1)

    def transform(table, field):
        return jnp.einsum("zr,crm->czm", table, field, precision=HIGHEST)

    items = lax.all_to_all(velocity, "planes", split_axis=2, concat_axis=1, tiled=True)
    values = transform(synth, items)
    along_z = transform(slope, items)
    shaped = values.reshape(values.shape[:-1] + (-1, QUAD * QUAD))
    along_r = jnp.einsum("...en,mn->...em", shaped, first, precision=HIGHEST).reshape(values.shape)
    along_s = jnp.einsum("...en,mn->...em", shaped, second, precision=HIGHEST).reshape(values.shape)
    along_x = geo_part[0] * along_r + geo_part[1] * along_s
    along_y = geo_part[2] * along_r + geo_part[3] * along_s
    values, along_x, along_y, along_z = (values, along_x, along_y, along_z)
    advection = values[0] * along_x + values[1] * along_y + values[2] * along_z
    advection_hat = jnp.einsum("rz,czm->crm", analysis, advection, precision=HIGHEST)
    returned = lax.all_to_all(advection_hat, "planes", split_axis=1, concat_axis=2, tiled=True)
    intermediate = velocity - STEP_DT * returned
    elem_count = element_kind.shape[0]
    row_count = 3 * local_rows
    waves = (
        (lax.axis_index("planes") * local_rows + jnp.arange(local_rows, dtype=jnp.int32) + 1) // 2
    ).astype(jnp.float32)
    lam = jnp.tile(SIGMA_COEF + (BETA_COEF * waves) ** 2, 3)
    free = (1 - dirichlet).astype(jnp.float32)[:, :, None, :]
    chooser = (element_kind == 1).astype(jnp.float32)

    def element_apply(vector, kinds, scales):
        flat = vector.reshape(vector.shape[0], -1)
        results = []
        for kind in range(2):
            stiff = jnp.dot(schur_stiffness[kind], flat, precision=HIGHEST).reshape(vector.shape)
            massed = jnp.dot(schur_mass[kind], flat, precision=HIGHEST).reshape(vector.shape)
            results.append(stiff + lam[None, :, None] * massed)
        return scales[None, None, :] * jnp.where(kinds[None, None, :] > 0.5, results[1], results[0])

    def element_vector(vertical, horizontal):
        arriving = passed_along(vertical[:, :, :COLUMN_ELEMS], "elem", -1)
        right = jnp.concatenate([vertical[:, :, COLUMN_ELEMS:], arriving], axis=2)
        grid = horizontal.reshape(horizontal.shape[0], horizontal.shape[1], -1, COLUMN_ELEMS)
        top = jnp.concatenate([grid[..., 1:], jnp.zeros_like(grid[..., :1])], axis=3).reshape(
            horizontal.shape
        )
        return jnp.concatenate([vertical, right, horizontal, top], axis=0)

    node_values = (SIGMA_COEF * intermediate).reshape(row_count, elem_count, QUAD * QUAD)
    lifted = jnp.where(
        chooser[None, None, :] > 0.5,
        jnp.einsum("kn,ren->kre", lift[1], node_values, precision=HIGHEST),
        jnp.einsum("kn,ren->kre", lift[0], node_values, precision=HIGHEST),
    )
    lifted_right = passed_along(lifted[QUAD : 2 * QUAD, :, -COLUMN_ELEMS:], "elem", 1)
    forcing = assemble(lifted, lifted_right, free)
    trace = (jnp.zeros_like(forcing[0]), jnp.zeros_like(forcing[1]))
    residual = forcing
    direction = forcing
    norm_now = global_squares(residual)
    for sweep in range(CG_STEPS):
        outputs = element_apply(element_vector(direction[0], direction[1]), chooser, element_scale)
        operator_arriving = passed_along(outputs[QUAD : 2 * QUAD, :, -COLUMN_ELEMS:], "elem", 1)
        image = assemble(outputs, operator_arriving, free)
        alpha = (norm_now / global_total(direction, image))[None, :, None]
        trace = (trace[0] + alpha * direction[0], trace[1] + alpha * direction[1])
        residual = (residual[0] - alpha * image[0], residual[1] - alpha * image[1])
        norm_next = global_squares(residual)
        ratio = (norm_next / norm_now)[None, :, None]
        direction = (residual[0] + ratio * direction[0], residual[1] + ratio * direction[1])
        norm_now = norm_next
    vector = element_vector(trace[0], trace[1])
    recovered = jnp.where(
        chooser[None, :, None] > 0.5,
        jnp.einsum("nl,lre->ren", recover[1], vector, precision=HIGHEST),
        jnp.einsum("nl,lre->ren", recover[0], vector, precision=HIGHEST),
    )
    weight = SIGMA_COEF / (SIGMA_COEF + lam)
    result = (
        intermediate.reshape(row_count, elem_count, QUAD * QUAD) * weight[:, None, None] + recovered
    )
    return result.reshape(velocity.shape)


LANES = 128
SUB = 16
F32 = jnp.float32
BF16 = jnp.bfloat16


def split(value):
    high = value.astype(BF16)
    return high, (value - high.astype(F32)).astype(BF16)


def np_split(value):
    high = np.asarray(value, np.float32).astype(BF16)
    low = (np.asarray(value, np.float64) - high.astype(np.float64)).astype(np.float32).astype(BF16)
    return high, low


def mm(first, second):
    return jnp.dot(first, second, preferred_element_type=F32)


def stacked_weights(weights):
    high, low = split(weights)
    return jnp.concatenate([high, high, low], axis=1)


def stacked_values(values):
    high, low = split(values)
    return jnp.concatenate([high, low, high], axis=0)


def advect_tables(planes):
    zeta = np.arange(planes)
    rows = np.arange(planes)
    waves = (rows + 1) // 2
    angle = 2.0 * np.pi / planes * ((waves[None, :] * zeta[:, None]) % planes)
    odd = (rows % 2 == 1)[None, :]
    first = (rows == 0)[None, :]
    last = (rows == planes - 1)[None, :]
    synth = np.where(first, 1.0, np.where(odd, np.cos(angle), np.sin(angle)))
    rate = BETA_COEF * waves[None, :]
    slope = np.where(first | last, 0.0, np.where(odd, -rate * np.sin(angle), rate * np.cos(angle)))
    weight = np.where((rows == 0) | (rows == planes - 1), 1.0 / planes, 2.0 / planes)
    analysis = synth.T * weight[:, None]
    high, low = np_split(np.concatenate([synth, slope], axis=0))
    forward = np.concatenate([high, high, low], axis=1)
    high, low = np_split(analysis)
    backward = np.concatenate([high, high, low], axis=1)
    points = QUAD * QUAD
    deriv = gauss_derivative(QUAD)
    both = np.zeros((LANES, 2 * LANES))
    both[:points, :points] = np.kron(deriv, np.eye(QUAD)).T
    both[:points, LANES : LANES + points] = np.kron(np.eye(QUAD), deriv).T
    high, low = np_split(both)
    return jnp.asarray(forward), jnp.asarray(backward), jnp.asarray(np.concatenate([high, high, low], axis=0))


def whole_spec(shape):
    return pl.BlockSpec(shape, lambda *_: (0,) * len(shape))


def params():
    return pltpu.CompilerParams(vmem_limit_bytes=60 * 1024 * 1024)


def solve_rows(own, other, own_fact, other_fact, lam, side_row, weights):
    half = own.shape[1]
    wide = 2 * half
    column = COLUMN_ELEMS // SUB * LANES
    second = jnp.concatenate([side_row] * (half // LANES), axis=1) > 0.5

    def joined(first, last):
        return jnp.concatenate([jnp.where(second, last, first), jnp.where(second, first, last)], axis=1)

    facts = joined(own_fact, other_fact)
    free_v = facts[:SUB]
    free_h = facts[SUB : 2 * SUB]
    is_second = facts[2 * SUB : 2 * SUB + 1] > 0.5
    scale = facts[2 * SUB + 1 : 2 * SUB + 2]
    w_all = stacked_weights(weights)
    lane = lax.broadcasted_iota(jnp.int32, (1, wide), 1)
    along = lane % LANES // SUB
    odd_half = lane // 8 % 2 == 1
    tile = lane // LANES
    per_column = COLUMN_ELEMS // SUB
    top_edge = (tile % per_column == per_column - 1) & odd_half & (along == SUB // 2 - 1)
    low_edge = (tile % per_column == 0) & jnp.logical_not(odd_half) & (along == 0)

    def above(x):
        last = jnp.where(odd_half, pltpu.roll(x, wide - 8, 1), pltpu.roll(x, 104, 1))
        moved = jnp.where(along < SUB // 2 - 1, pltpu.roll(x, wide - 16, 1), last)
        return jnp.where(top_edge, 0.0, moved)

    def below(x):
        head = jnp.where(odd_half, pltpu.roll(x, wide - 104, 1), pltpu.roll(x, 8, 1))
        moved = jnp.where(along > 0, pltpu.roll(x, 16, 1), head)
        return jnp.where(low_edge, 0.0, moved)

    edge = jnp.zeros((SUB, column), F32)

    def vector_of(v, h):
        right = jnp.concatenate([v[:, column:], edge], axis=1)
        return jnp.concatenate([v, right, h, above(h)], axis=0)

    def gather(parts):
        right = jnp.concatenate([edge, parts[SUB : 2 * SUB, :-column]], axis=1)
        v = (parts[:SUB] + right) * free_v
        h = (parts[2 * SUB : 3 * SUB] + below(parts[3 * SUB :])) * free_h
        return v, h

    def total(product):
        acc = product[:, :LANES]
        for at in range(1, wide // LANES):
            acc = acc + product[:, at * LANES : (at + 1) * LANES]
        acc = jnp.sum(acc, axis=0, keepdims=True)
        acc = jnp.broadcast_to(acc, (8, LANES))
        for step in (8, 16, 32, 64):
            acc = acc + pltpu.roll(acc, step, 1)
        return acc[0:1]

    def spread(row):
        return jnp.concatenate([row] * (wide // LANES), axis=1)

    res_v, res_h = gather(joined(own, other))
    now = total(res_v * res_v + res_h * res_h)
    zero = jnp.zeros_like(res_v)

    def sweep(_, state):
        tr_v, tr_h, res_v, res_h, dir_v, dir_h, now = state
        both = mm(w_all, stacked_values(vector_of(dir_v, dir_h)))
        rows = 4 * SUB
        stiff = jnp.where(is_second, both[rows : 2 * rows], both[:rows])
        mass = jnp.where(is_second, both[3 * rows :], both[2 * rows : 3 * rows])
        im_v, im_h = gather(scale * (stiff + lam * mass))
        alpha = spread(now / total(dir_v * im_v + dir_h * im_h))
        tr_v, tr_h = tr_v + alpha * dir_v, tr_h + alpha * dir_h
        res_v, res_h = res_v - alpha * im_v, res_h - alpha * im_h
        fresh = total(res_v * res_v + res_h * res_h)
        ratio = spread(fresh / now)
        return tr_v, tr_h, res_v, res_h, res_v + ratio * dir_v, res_h + ratio * dir_h, fresh

    state = lax.fori_loop(0, CG_STEPS, sweep, (zero, zero, res_v, res_h, res_v, res_h, now))
    vector = vector_of(state[0], state[1])
    mine = jnp.where(second, vector[:, half:], vector[:, :half])
    away = jnp.where(second, vector[:, :half], vector[:, half:])
    return mine, away


def advect_and_solve(velocity, geometry, lift_rows, kind_lanes, side, facts, lam_lanes, matrices, count):
    comps, rows, nodes = velocity.shape
    points = QUAD * QUAD
    per = LANES // rows
    pairs = per // 2
    planes = count * rows
    half = count * LANES // 2
    forward, backward, deriv = advect_tables(planes)

    def kernel(
        vel_ref, geo, forward_ref, backward_ref, deriv_ref, lift_ref, kinds, side_ref, facts_ref, lam_ref, mat_ref,
        mid, mine_out, other_out,
        sent, recv, hats, ret, store, fields, slopes, own, away, other, traces, their_traces, facts_out, their_facts,
        send_sem, recv_sem, pair_send, pair_recv,
    ):
        me = lax.axis_index("planes")
        core = lax.axis_index("elem")
        barrier = pltpu.get_barrier_semaphore()

        def greet(step, carry):
            pl.semaphore_signal(
                barrier, inc=1, device_id={"planes": lax.rem(me + step, count)}, device_id_type=pl.DeviceIdType.MESH
            )
            return carry

        lax.fori_loop(1, count, greet, 0)
        pl.semaphore_signal(barrier, inc=1, device_id={"elem": 1 - core}, device_id_type=pl.DeviceIdType.MESH)

        def copy_to(source, target, way, comp, peer):
            return pltpu.make_async_remote_copy(
                src_ref=source.at[comp, peer],
                dst_ref=target.at[comp, me],
                send_sem=send_sem.at[way, comp, peer],
                recv_sem=recv_sem.at[way, comp, me],
                device_id={"planes": peer},
                device_id_type=pl.DeviceIdType.MESH,
            )

        def copy_from(source, target, way, comp, peer):
            return pltpu.make_async_remote_copy(
                src_ref=source.at[comp, peer],
                dst_ref=target.at[comp, peer],
                send_sem=send_sem.at[way, comp, peer],
                recv_sem=recv_sem.at[way, comp, peer],
                device_id={"planes": peer},
                device_id_type=pl.DeviceIdType.MESH,
            )

        def start_all(source, target, way, comp):
            def one(step, carry):
                copy_to(source, target, way, comp, lax.rem(me + count // 2 + step, count)).start()
                return carry

            lax.fori_loop(0, count // 2, one, 0)

            def two(step, carry):
                copy_to(source, target, way, comp, lax.rem(me + step, count)).start()
                return carry

            lax.fori_loop(1, count // 2, two, 0)

        def pair_copy(source, target, at):
            return pltpu.make_async_remote_copy(
                src_ref=source,
                dst_ref=target,
                send_sem=pair_send.at[at],
                recv_sem=pair_recv.at[at],
                device_id={"elem": 1 - core},
                device_id_type=pl.DeviceIdType.MESH,
            )

        def pack(comp):
            for part in range(count):
                pieces = []
                for local in range(per):
                    at = (part * per + local) * points
                    pieces.append(vel_ref[comp, :, at : at + points])
                sent[comp, part] = jnp.concatenate(pieces, axis=0).T

        def arrive(comp, part, block):
            block = jnp.concatenate([block, jnp.zeros((LANES - points, LANES), F32)], axis=0).T
            for local in range(per):
                at = local % 2 * LANES
                store[local // 2, pl.ds(pl.multiple_of(part * rows, rows), rows), at : at + LANES] = block[
                    local * rows : (local + 1) * rows
                ]

        def arrive_all(comp):
            arrive(comp, me, sent[comp, me])

            def one(step, carry):
                part = lax.rem(me + step, count)
                copy_from(sent, recv, 0, comp, part).wait_recv()
                arrive(comp, part, recv[comp, part])
                return carry

            lax.fori_loop(count // 2, count, one, 0)
            lax.fori_loop(1, count // 2, one, 0)

        def synthesize(comp):
            def one(pair, carry):
                field = mm(forward_ref[...], stacked_values(store[pair]))
                fields[comp, pair] = field
                for which in range(2):
                    high, low = split(field[:planes, which * LANES : (which + 1) * LANES])
                    slopes[comp, pair, which] = mm(jnp.concatenate([high, low], axis=1), deriv_ref[: 2 * LANES]) + mm(
                        high, deriv_ref[2 * LANES :]
                    )
                return carry

            lax.fori_loop(0, pairs, one, 0)

        def advect(comp):
            def one(pair, carry):
                results = []
                for which in range(2):
                    at = slice(which * LANES, (which + 1) * LANES)
                    vel = [fields[item, pair, :planes, at] for item in range(comps)]
                    part = geo[pair * 2 + which]
                    results.append(
                        slopes[comp, pair, which, :, :LANES] * (vel[0] * part[0:1] + vel[1] * part[2:3])
                        + slopes[comp, pair, which, :, LANES:] * (vel[0] * part[1:2] + vel[1] * part[3:4])
                        + vel[2] * fields[comp, pair, planes:, at]
                    )
                store[pair] = mm(backward_ref[...], stacked_values(jnp.concatenate(results, axis=1)))
                return carry

            lax.fori_loop(0, pairs, one, 0)
            for part in range(count):
                block = jnp.concatenate(
                    [
                        store[local // 2, part * rows : (part + 1) * rows, local % 2 * LANES : (local % 2 + 1) * LANES]
                        for local in range(per)
                    ],
                    axis=0,
                )
                hats[comp, part] = block.T[:points]

        def lift(comp):
            def one(step, carry):
                copy_from(hats, ret, 1, comp, lax.rem(me + step, count)).wait_recv()
                return carry

            lax.fori_loop(1, count, one, 0)
            ret[comp, me] = hats[comp, me]
            for part in range(count):
                mid[comp, part] = sent[comp, part] - STEP_DT * ret[comp, part]
            field = jnp.concatenate([mid[comp, part] for part in range(count)], axis=1)
            high, low = split(SIGMA_COEF * field)
            w_high, w_low = split(lift_ref[...])
            both = mm(w_high, high) + (mm(w_high, low) + mm(w_low, high))
            lifted = jnp.where(kinds[0:1] > 0.5, both[4 * SUB :], both[: 4 * SUB])
            bit = lax.broadcasted_iota(jnp.int32, (4 * SUB, LANES), 1) // 8 % 2 == 0
            second = side_ref[0:1] > 0.5
            for tile in range(count // 2):
                even = lifted[:, 2 * tile * LANES : (2 * tile + 1) * LANES]
                odd = lifted[:, (2 * tile + 1) * LANES : (2 * tile + 2) * LANES]
                low_rows = jnp.where(bit, even, pltpu.roll(odd, 8, 1))
                high_rows = jnp.where(bit, pltpu.roll(even, LANES - 8, 1), odd)
                at = slice(tile * LANES, (tile + 1) * LANES)
                own[comp, :, at] = jnp.where(second, high_rows, low_rows)
                away[comp, :, at] = jnp.where(second, low_rows, high_rows)
            pair_copy(away.at[comp], other.at[comp], comp).start()

        def solve(comp):
            pair_copy(away.at[comp], other.at[comp], comp).wait_recv()
            mine, theirs = solve_rows(
                own[comp], other[comp], facts_ref[...], their_facts[...], lam_ref[0:1], side_ref[0:1], mat_ref[...]
            )
            mine_out[comp] = mine
            traces[comp] = theirs
            pair_copy(traces.at[comp], their_traces.at[comp], comps + comp).start()

        facts_out[...] = facts_ref[...]
        pack(0)
        pl.semaphore_wait(barrier, count)
        start_all(sent, recv, 0, 0)
        pair_copy(facts_out, their_facts, 2 * comps).start()
        for comp in range(1, comps):
            pack(comp)
            start_all(sent, recv, 0, comp)
        for comp in range(comps):
            arrive_all(comp)
            synthesize(comp)
        for comp in range(comps):
            advect(comp)
            start_all(hats, ret, 1, comp)
        pair_copy(facts_out, their_facts, 2 * comps).wait_recv()
        for comp in range(comps):
            lift(comp)
            solve(comp)
        for comp in range(comps):
            pair_copy(traces.at[comp], their_traces.at[comp], comps + comp).wait_recv()
            other_out[comp] = their_traces[comp]
        pair_copy(facts_out, their_facts, 2 * comps).wait_send()
        for comp in range(comps):
            pair_copy(away.at[comp], other.at[comp], comp).wait_send()
            pair_copy(traces.at[comp], their_traces.at[comp], comps + comp).wait_send()

            def drain(step, carry):
                peer = lax.rem(me + step, count)
                copy_to(sent, recv, 0, comp, peer).wait_send()
                copy_to(hats, ret, 1, comp, peer).wait_send()
                return carry

            lax.fori_loop(1, count, drain, 0)

    message = (comps, count, points, LANES)
    piece = (comps, 4 * SUB, half)
    operands = (velocity, geometry, forward, backward, deriv, lift_rows, kind_lanes, side, facts, lam_lanes, matrices)
    vmem = pl.BlockSpec(memory_space=pltpu.VMEM)
    return pl.pallas_call(
        kernel,
        in_specs=[vmem] * len(operands),
        out_specs=[vmem] * 3,
        out_shape=[
            jax.ShapeDtypeStruct(message, F32),
            jax.ShapeDtypeStruct(piece, F32),
            jax.ShapeDtypeStruct(piece, F32),
        ],
        scratch_shapes=[pltpu.VMEM(message, F32)] * 4
        + [
            pltpu.VMEM((pairs, planes, 2 * LANES), F32),
            pltpu.VMEM((comps, pairs, 2 * planes, 2 * LANES), F32),
            pltpu.VMEM((comps, pairs, 2, planes, 2 * LANES), F32),
        ]
        + [pltpu.VMEM(piece, F32)] * 5
        + [pltpu.VMEM(facts.shape, F32)] * 2
        + [
            pltpu.SemaphoreType.DMA((2, comps, count)),
            pltpu.SemaphoreType.DMA((2, comps, count)),
            pltpu.SemaphoreType.DMA((2 * comps + 1,)),
            pltpu.SemaphoreType.DMA((2 * comps + 1,)),
        ],
        compiler_params=pltpu.CompilerParams(
            vmem_limit_bytes=60 * 1024 * 1024, collective_id=0, has_side_effects=True
        ),
        name="advect_and_solve",
    )(*operands)


def recover_nodes(mid, mine, other, side, kind_lanes, weight_lanes, recover_cols, rows):
    comps, count, points, _ = mid.shape
    half = mine.shape[2]
    per = LANES // rows
    nodes = count * per * points
    second_at = recover_cols.shape[0] // 2

    def kernel(mid_ref, mine_ref, other_ref, side_ref, kinds, factor, weights, out):
        second = side_ref[0:1] > 0.5
        bit = lax.broadcasted_iota(jnp.int32, (4 * SUB, LANES), 1) // 8 % 2 == 0
        tiles = []
        for tile in range(half // LANES):
            at = slice(tile * LANES, (tile + 1) * LANES)
            first_half = mine_ref[0, :, at]
            last_half = other_ref[0, :, at]
            low_rows = jnp.where(second, last_half, first_half)
            high_rows = jnp.where(second, first_half, last_half)
            tiles.append(jnp.where(bit, low_rows, pltpu.roll(high_rows, 8, 1)))
            tiles.append(jnp.where(bit, pltpu.roll(low_rows, LANES - 8, 1), high_rows))
        both = mm(stacked_weights(weights[...]), stacked_values(jnp.concatenate(tiles, axis=1)))
        found = jnp.where(kinds[0:1] > 0.5, both[second_at : second_at + points], both[:points])
        for part in range(count):
            at = slice(part * LANES, (part + 1) * LANES)
            block = mid_ref[0, part] * factor[0:1, at] + found[:, at]
            block = jnp.concatenate([block, jnp.zeros((LANES - points, LANES), F32)], axis=0).T
            for local in range(per):
                start = (part * per + local) * points
                out[0, :, start : start + points] = block[local * rows : (local + 1) * rows, :points]

    piece = pl.BlockSpec((1, 4 * SUB, half), lambda c: (c, 0, 0))
    extra = (side, kind_lanes, weight_lanes, recover_cols)
    return pl.pallas_call(
        kernel,
        grid=(comps,),
        in_specs=[pl.BlockSpec((1, count, points, LANES), lambda c: (c, 0, 0, 0)), piece, piece]
        + [whole_spec(item.shape) for item in extra],
        out_specs=pl.BlockSpec((1, rows, nodes), lambda c: (c, 0, 0)),
        out_shape=jax.ShapeDtypeStruct((comps, rows, nodes), F32),
        compiler_params=params(),
        name="recover_nodes",
    )(mid, mine, other, *extra)


def edge_rows(matrix):
    shape = matrix.shape
    grouped = matrix.reshape(shape[0], 4, QUAD, shape[2])
    grouped = jnp.pad(grouped, ((0, 0), (0, 0), (0, SUB - QUAD), (0, 0)))
    return grouped.reshape(shape[0], 4 * SUB, shape[2])


def edge_cols(matrix):
    return edge_rows(matrix.swapaxes(1, 2)).swapaxes(1, 2)


def fast_device(
    velocity,
    geometry,
    element_kind,
    element_scale,
    dirichlet,
    schur_stiffness,
    schur_mass,
    lift,
    recover,
):
    count = lax.axis_size("planes")
    rows = velocity.shape[1]
    elems = element_kind.shape[0]
    points = QUAD * QUAD
    per = elems // count
    core = lax.axis_index("elem")
    place = lax.axis_index("planes")
    side = jnp.broadcast_to(core.astype(F32), (8, LANES))

    free = jnp.pad((1 - dirichlet).astype(F32), ((0, 0), (0, SUB - QUAD), (0, 0))).reshape(2 * SUB, elems)
    facts = jnp.concatenate(
        [free, (element_kind == 1).astype(F32)[None], element_scale[None], jnp.zeros((6, elems), F32)], axis=0
    )
    facts = facts.reshape(facts.shape[0], elems // 16, 2, 8).swapaxes(2, 3)
    facts = jnp.broadcast_to(facts[..., None], facts.shape + (8,)).reshape(facts.shape[0], elems * 8)

    def lam_of(row):
        return SIGMA_COEF + (BETA_COEF * ((row + 1) // 2).astype(F32)) ** 2

    lane = jnp.arange(count * LANES, dtype=jnp.int32)
    lam_half = lam_of(place * rows + core * 8 + lane % 8)
    lam_lanes = jnp.broadcast_to(lam_half[None], (8, lane.shape[0]))
    weight = SIGMA_COEF / (SIGMA_COEF + lam_of(place * rows + lane % rows))
    weight_lanes = jnp.broadcast_to(weight[None], (8, lane.shape[0]))
    kinds = jnp.broadcast_to((element_kind == 1).astype(F32)[None, :, None], (8, elems, rows)).reshape(8, elems * rows)
    geo = lax.dynamic_slice_in_dim(geometry.reshape(4, elems, points), place * per, per, 1)
    geo = jnp.pad(geo.swapaxes(0, 1), ((0, 0), (0, 4), (0, LANES - points)))

    lift_rows = edge_rows(lift).reshape(8 * SUB, points)
    matrices = jnp.concatenate([schur_stiffness, schur_mass], axis=0)
    matrices = edge_cols(edge_rows(matrices)).reshape(16 * SUB, 4 * SUB)
    recover_cols = jnp.pad(edge_cols(recover), ((0, 0), (0, 88 - points), (0, 0))).reshape(2 * 88, 4 * SUB)
    mid, mine, other = advect_and_solve(velocity, geo, lift_rows, kinds, side, facts, lam_lanes, matrices, count)
    return recover_nodes(mid, mine, other, side, kinds, weight_lanes, recover_cols, rows)


def per_device(velocity, geometry, element_kind, *rest):
    count = lax.axis_size("planes")
    rows = velocity.shape[1]
    elems = element_kind.shape[0]
    fits = rows == 16 and elems == LANES and elems * rows == count * LANES and lax.axis_size("elem") == 2
    body = fast_device if fits else plain_device
    return body(velocity, geometry, element_kind, *rest)


def solution(mesh):
    in_specs = (
        P(None, "planes", "elem"),
        P(None, "elem"),
        P("elem"),
        P("elem"),
        P(None, None, "elem"),
        P(),
        P(),
        P(),
        P(),
    )
    out_specs = P(None, "planes", "elem")
    return jax.shard_map(
        per_device, mesh=mesh, in_specs=in_specs, out_specs=out_specs, check_vma=False
    )
```

profile of v0, /device:TPU:1, one launch (start us, length us, event | category | flops | bytes accessed | tf_op | source)
XLA Modules:
  0.0 136.9 jit_solution(15723899210705646412)
XLA Ops:
  0.0 0.0 copy-start
  0.0 0.7 compare_convert_fusion
  0.7 0.1 pad.39.clone
  0.8 0.6 broadcast_in_dim.19.side_ref
  1.4 0.7 subtract_convert_fusion
  2.1 0.6 broadcast_in_dim.42.lam_ref
  2.7 0.6 broadcast_in_dim.43.factor
  3.4 0.2 concatenate.18
  3.6 0.1 broadcast_in_dim.16
  3.6 0.1 broadcast_in_dim.17
  3.7 0.6 broadcast_in_dim.18.kinds
  4.4 0.8 concatenate.19
  5.2 0.8 copy.31
  6.0 0.6 pad.28
  6.6 0.8 copy.46
  7.4 0.1 copy.47
  7.5 0.6 pad.33.clone
  8.2 0.8 pad_maximum_fusion
  9.1 0.1 copy.37
  9.2 0.8 copy.39
  10.0 0.1 copy.44
  10.2 0.1 concatenate.13
  10.3 0.1 maximum_bitcast_fusion
  10.4 0.0 copy-done
  10.4 0.3 reshape.107
  10.8 0.6 pad.27.geo
  11.5 0.8 copy.40.facts_ref
  12.3 118.8 %advect_and_solve.1 = (f32[3,16,81,128]{3,2,1,0:T(8,128)}, f32[3,64,1024]{2,1,0:T(8,128)}, f32[3,64,1024]{2,1,0:T(8,128)}) custom-call(f32[3,16,10368]{2,1,0:T(8,128)} %vel_ref.1, f32[8,8,128]{2,1,0:T(8,128)} %pad.27.geo, bf16[512,768]{1,0:T(8,128)(2,1)} %constant.77.clone.forward_ref, bf16[256,768]{1,0:T(8,128)(2,1)} %constant.78.clone.backward_ref, ...), custom_call_target="tpu_custom_call" | custom-call | tf_op jit(solution)/shard_map/advect_and_solve/pallas_call | solution.py:553
  131.1 5.7 %recover_nodes.1 = f32[3,16,10368]{2,1,0:T(8,128)} custom-call(f32[3,16,81,128]{3,2,1,0:T(8,128)} %get-tuple-element.8.mid_ref, f32[3,64,1024]{2,1,0:T(8,128)} %get-tuple-element.9.mine_ref, f32[3,64,1024]{2,1,0:T(8,128)} %get-tuple-element.10.other_ref, f32[8,128]{1,0:T(8,128)} %broadcast_in_dim.19.side_ref, f32[8,2048]{1,0:T(8,128)} %broadcast_in_dim.18.kinds, ...), custom_call_target="tpu_custom_call" | custom-call | tf_op jit(solution)/shard_map/recover_nodes/pallas_call | solution.py:614
  (13 shorter events, 0.2 us)
Async XLA Ops:
  0.0 10.4 %copy-start = (f32[4,10368]{1,0:T(4,128)S(1)}, f32[4,10368]{1,0:T(4,128)}, u32[]{:S(2)}) copy-start(f32[4,10368]{1,0:T(4,128)} %param.13) | copy-start | bytes 497668
where the time goes:
time: 137 us
  Pallas kernels  125 us (91%)
  local copies, waits for them, and re-layouts  9.8 us (7%)
  other arithmetic  2.37 us (2%)
    pallas_call x1, Pallas kernels, advect_and_solve(): pl.pallas_call(kernel, in_specs=[vmem] * len(operands), out_specs=[vmem]...  119 us
    pallas_call x1, Pallas kernels, recover_nodes(): pl.pallas_call(kernel, grid=(comps,), in_specs=[pl.BlockSpec((1, count, p...  5.74 us

commit v1 on v0

--- a/solution.py
+++ b/solution.py
@@ -339,7 +339,20 @@
     return mine, away
 
 
-def advect_and_solve(velocity, geometry, lift_rows, kind_lanes, side, facts, lam_lanes, matrices, count):
+def exact(first, second):
+    return jnp.dot(first, second, precision=HIGHEST, preferred_element_type=F32)
+
+
+def iota(shape, axis):
+    return lax.broadcasted_iota(jnp.int32, shape, axis)
+
+
+def lam_of(row):
+    return SIGMA_COEF + (BETA_COEF * ((row + 1) // 2).astype(F32)) ** 2
+
+
+def advect_and_solve(velocity, geometry, kind, scale, dirichlet, stiffness, mass, lift_maps, recover_maps, count):
+    elems = kind.shape[1]
     comps, rows, nodes = velocity.shape
     points = QUAD * QUAD
     per = LANES // rows
@@ -349,9 +362,11 @@
     forward, backward, deriv = advect_tables(planes)
 
     def kernel(
-        vel_ref, geo, forward_ref, backward_ref, deriv_ref, lift_ref, kinds, side_ref, facts_ref, lam_ref, mat_ref,
-        mid, mine_out, other_out,
+        vel_ref, geo_ref, kind_ref, scale_ref, fixed_ref, stiff_ref, mass_ref, lift_in, recover_in,
+        forward_ref, backward_ref, deriv_ref,
+        mid, mine_out, other_out, kinds, factor, recover_out, side_ref,
         sent, recv, hats, ret, store, fields, slopes, own, away, other, traces, their_traces, facts_out, their_facts,
+        geo, lift_ref, mat_ref, lam_ref,
         send_sem, recv_sem, pair_send, pair_recv,
     ):
         me = lax.axis_index("planes")
@@ -440,10 +455,15 @@
 
         def synthesize(comp):
             def one(pair, carry):
-                field = mm(forward_ref[...], stacked_values(store[pair]))
-                fields[comp, pair] = field
+                fields[comp, pair] = mm(forward_ref[...], stacked_values(store[pair]))
+                return carry
+
+            lax.fori_loop(0, pairs, one, 0)
+
+        def derive(comp):
+            def one(pair, carry):
                 for which in range(2):
-                    high, low = split(field[:planes, which * LANES : (which + 1) * LANES])
+                    high, low = split(fields[comp, pair, :planes, which * LANES : (which + 1) * LANES])
                     slopes[comp, pair, which] = mm(jnp.concatenate([high, low], axis=1), deriv_ref[: 2 * LANES]) + mm(
                         high, deriv_ref[2 * LANES :]
                     )
@@ -506,24 +526,69 @@
         def solve(comp):
             pair_copy(away.at[comp], other.at[comp], comp).wait_recv()
             mine, theirs = solve_rows(
-                own[comp], other[comp], facts_ref[...], their_facts[...], lam_ref[0:1], side_ref[0:1], mat_ref[...]
+                own[comp], other[comp], facts_out[...], their_facts[...], lam_ref[0:1], side_ref[0:1], mat_ref[...]
             )
             mine_out[comp] = mine
             traces[comp] = theirs
             pair_copy(traces.at[comp], their_traces.at[comp], comps + comp).start()
 
-        facts_out[...] = facts_ref[...]
+        def prepare():
+            group = iota((4 * SUB, 4 * QUAD), 0)
+            place = group // SUB * QUAD + group % SUB
+            widen = ((place == iota((4 * SUB, 4 * QUAD), 1)) & (group % SUB < QUAD)).astype(F32)
+            group = iota((4 * QUAD, 4 * SUB), 1)
+            place = group // SUB * QUAD + group % SUB
+            widen_cols = ((place == iota((4 * QUAD, 4 * SUB), 0)) & (group % SUB < QUAD)).astype(F32)
+            recover_out[...] = jnp.zeros_like(recover_out)
+            for which in range(2):
+                at = which * 4 * SUB
+                mat_ref[at : at + 4 * SUB] = exact(exact(widen, stiff_ref[:, which, :]), widen_cols)
+                at = at + 8 * SUB
+                mat_ref[at : at + 4 * SUB] = exact(exact(widen, mass_ref[:, which, :]), widen_cols)
+                lift_ref[which * 4 * SUB : (which + 1) * 4 * SUB] = exact(widen, lift_in[:, which, :])
+                recover_out[which * 88 : which * 88 + points] = exact(widen, recover_in[:, which, :]).T
+            is_second = (kind_ref[...] == 1).astype(F32)
+            pad = jnp.zeros((SUB - QUAD, elems), F32)
+            free_v = (1 - fixed_ref[:, 0, :]).astype(F32)
+            free_h = (1 - fixed_ref[:, 1, :]).astype(F32)
+            table = jnp.concatenate(
+                [free_v, pad, free_h, pad, is_second, scale_ref[...], jnp.zeros((6, elems), F32)], axis=0
+            )
+            lane = iota((elems, half), 1)
+            element = lane // LANES * 16 + lane // 8 % 2 * 8 + lane % LANES // 16
+            facts_out[...] = exact(table, (element == iota((elems, half), 0)).astype(F32))
+            lane = iota((elems, 2 * half), 1)
+            spread = (lane // rows == iota((elems, 2 * half), 0)).astype(F32)
+            kinds[...] = exact(jnp.broadcast_to(is_second, (8, elems)), spread)
+            lane = iota((8, 2 * half), 1)
+            lam_ref[...] = lam_of(me * rows + core * 8 + lane % 8)
+            factor[...] = SIGMA_COEF / (SIGMA_COEF + lam_of(me * rows + lane % rows))
+            side_ref[...] = jnp.full((8, LANES), core, jnp.int32).astype(F32)
+            geo[...] = jnp.zeros_like(geo)
+            for part in range(count):
+
+                @pl.when(me == part)
+                def _():
+                    for local in range(per):
+                        at = (part * per + local) * points
+                        geo[local, 0:4, 0:points] = geo_ref[:, at : at + points]
+
         pack(0)
         pl.semaphore_wait(barrier, count)
         start_all(sent, recv, 0, 0)
-        pair_copy(facts_out, their_facts, 2 * comps).start()
         for comp in range(1, comps):
             pack(comp)
             start_all(sent, recv, 0, comp)
+        prepare()
+        pair_copy(facts_out, their_facts, 2 * comps).start()
         for comp in range(comps):
             arrive_all(comp)
             synthesize(comp)
+            if comp < comps - 1:
+                derive(comp)
         for comp in range(comps):
+            if comp == comps - 1:
+                derive(comp)
             advect(comp)
             start_all(hats, ret, 1, comp)
         pair_copy(facts_out, their_facts, 2 * comps).wait_recv()
@@ -548,16 +613,22 @@
 
     message = (comps, count, points, LANES)
     piece = (comps, 4 * SUB, half)
-    operands = (velocity, geometry, forward, backward, deriv, lift_rows, kind_lanes, side, facts, lam_lanes, matrices)
+    operands = (velocity, geometry, kind, scale, dirichlet, stiffness, mass, lift_maps, recover_maps)
+    operands = operands + (forward, backward, deriv)
+    facts = pltpu.VMEM((40, half), F32)
     vmem = pl.BlockSpec(memory_space=pltpu.VMEM)
     return pl.pallas_call(
         kernel,
         in_specs=[vmem] * len(operands),
-        out_specs=[vmem] * 3,
+        out_specs=[vmem] * 7,
         out_shape=[
             jax.ShapeDtypeStruct(message, F32),
             jax.ShapeDtypeStruct(piece, F32),
             jax.ShapeDtypeStruct(piece, F32),
+            jax.ShapeDtypeStruct((8, 2 * half), F32),
+            jax.ShapeDtypeStruct((8, 2 * half), F32),
+            jax.ShapeDtypeStruct((2 * 88, 4 * SUB), F32),
+            jax.ShapeDtypeStruct((8, LANES), F32),
         ],
         scratch_shapes=[pltpu.VMEM(message, F32)] * 4
         + [
@@ -566,7 +637,14 @@
             pltpu.VMEM((comps, pairs, 2, planes, 2 * LANES), F32),
         ]
         + [pltpu.VMEM(piece, F32)] * 5
-        + [pltpu.VMEM(facts.shape, F32)] * 2
+        + [
+            facts,
+            facts,
+            pltpu.VMEM((per, 8, LANES), F32),
+            pltpu.VMEM((8 * SUB, points), F32),
+            pltpu.VMEM((16 * SUB, 4 * SUB), F32),
+            pltpu.VMEM((8, 2 * half), F32),
+        ]
         + [
             pltpu.SemaphoreType.DMA((2, comps, count)),
             pltpu.SemaphoreType.DMA((2, comps, count)),
@@ -623,17 +701,6 @@
     )(mid, mine, other, *extra)
 
 
-def edge_rows(matrix):
-    shape = matrix.shape
-    grouped = matrix.reshape(shape[0], 4, QUAD, shape[2])
-    grouped = jnp.pad(grouped, ((0, 0), (0, 0), (0, SUB - QUAD), (0, 0)))
-    return grouped.reshape(shape[0], 4 * SUB, shape[2])
-
-
-def edge_cols(matrix):
-    return edge_rows(matrix.swapaxes(1, 2)).swapaxes(1, 2)
-
-
 def fast_device(
     velocity,
     geometry,
@@ -646,39 +713,19 @@
     recover,
 ):
     count = lax.axis_size("planes")
-    rows = velocity.shape[1]
-    elems = element_kind.shape[0]
-    points = QUAD * QUAD
-    per = elems // count
-    core = lax.axis_index("elem")
-    place = lax.axis_index("planes")
-    side = jnp.broadcast_to(core.astype(F32), (8, LANES))
-
-    free = jnp.pad((1 - dirichlet).astype(F32), ((0, 0), (0, SUB - QUAD), (0, 0))).reshape(2 * SUB, elems)
-    facts = jnp.concatenate(
-        [free, (element_kind == 1).astype(F32)[None], element_scale[None], jnp.zeros((6, elems), F32)], axis=0
-    )
-    facts = facts.reshape(facts.shape[0], elems // 16, 2, 8).swapaxes(2, 3)
-    facts = jnp.broadcast_to(facts[..., None], facts.shape + (8,)).reshape(facts.shape[0], elems * 8)
-
-    def lam_of(row):
-        return SIGMA_COEF + (BETA_COEF * ((row + 1) // 2).astype(F32)) ** 2
-
-    lane = jnp.arange(count * LANES, dtype=jnp.int32)
-    lam_half = lam_of(place * rows + core * 8 + lane % 8)
-    lam_lanes = jnp.broadcast_to(lam_half[None], (8, lane.shape[0]))
-    weight = SIGMA_COEF / (SIGMA_COEF + lam_of(place * rows + lane % rows))
-    weight_lanes = jnp.broadcast_to(weight[None], (8, lane.shape[0]))
-    kinds = jnp.broadcast_to((element_kind == 1).astype(F32)[None, :, None], (8, elems, rows)).reshape(8, elems * rows)
-    geo = lax.dynamic_slice_in_dim(geometry.reshape(4, elems, points), place * per, per, 1)
-    geo = jnp.pad(geo.swapaxes(0, 1), ((0, 0), (0, 4), (0, LANES - points)))
-
-    lift_rows = edge_rows(lift).reshape(8 * SUB, points)
-    matrices = jnp.concatenate([schur_stiffness, schur_mass], axis=0)
-    matrices = edge_cols(edge_rows(matrices)).reshape(16 * SUB, 4 * SUB)
-    recover_cols = jnp.pad(edge_cols(recover), ((0, 0), (0, 88 - points), (0, 0))).reshape(2 * 88, 4 * SUB)
-    mid, mine, other = advect_and_solve(velocity, geo, lift_rows, kinds, side, facts, lam_lanes, matrices, count)
-    return recover_nodes(mid, mine, other, side, kinds, weight_lanes, recover_cols, rows)
+    mid, mine, other, kinds, factor, recover_cols, side = advect_and_solve(
+        velocity,
+        geometry,
+        element_kind[None],
+        element_scale[None],
+        dirichlet.swapaxes(0, 1),
+        schur_stiffness.swapaxes(0, 1),
+        schur_mass.swapaxes(0, 1),
+        lift.swapaxes(0, 1),
+        recover.transpose(2, 0, 1),
+        count,
+    )
+    return recover_nodes(mid, mine, other, side, kinds, factor, recover_cols, velocity.shape[1])
 
 
 def per_device(velocity, geometry, element_kind, *rest):

time: 137 us -> 123 us (0.90)
  local copies, waits for them, and re-layouts: 9.8 us -> 0 us
  other arithmetic: 2.37 us -> 0 us
  Pallas kernels: 125 us -> 123 us
    broadcast_in_dim x8 -> x0, local copies, waits for them, and re-layouts: 2.67 us -> none  [the longest x3 0.8 us: fast_device(): jnp.broadcast_to((element_kind == 1).astype(F32)[None, :, None], (8, elem...]
    pad x7 -> x0, local copies, waits for them, and re-layouts: 1.98 us -> none  [the longest x4 0.68 us: edge_rows(): grouped = jnp.pad(grouped, ((0, 0), (0, 0), (0, SUB - QUAD), (0, 0)))]
    reshape x4 -> x0, local copies, waits for them, and re-layouts: 1.96 us -> none  [the longest x1 0.85 us: fast_device(): jnp.broadcast_to(facts[..., None], facts.shape + (8,))]
    pallas_call x1, Pallas kernels: 119 us -> 117 us  [advect_and_solve(): pl.pallas_call(kernel, in_specs=[vmem] * len(operands), out_specs=[vmem]...]
    convert_element_type x2 -> x0, other arithmetic: 1.4 us -> none  [the longest x1 0.71 us: fast_device(): (1 - dirichlet).astype(F32)]
where the time goes in v1:
time: 123 us
  Pallas kernels  123 us (100%)
    pallas_call x1, Pallas kernels, advect_and_solve(): pl.pallas_call(kernel, in_specs=[vmem] * len(operands), out_specs=[vmem]...  117 us
    pallas_call x1, Pallas kernels, recover_nodes(): pl.pallas_call(kernel, grid=(comps,), in_specs=[pl.BlockSpec((1, count, p...  5.73 us

profile of v1, /device:TPU:1, one launch (start us, length us, event | category | flops | bytes accessed | tf_op | source)
XLA Modules:
  0.0 123.1 jit_solution(222543196739315784)
XLA Ops:
  0.0 117.3 %advect_and_solve.1 = (f32[3,16,81,128]{3,2,1,0:T(8,128)}, f32[3,64,1024]{2,1,0:T(8,128)}, f32[3,64,1024]{2,1,0:T(8,128)}, f32[8,2048]{1,0:T(8,128)}, f32[8,2048...) custom-call(f32[3,16,10368]{2,1,0:T(8,128)} %vel_ref.1, f32[4,10368]{1,0:T(4,128)} %geo_ref.1, s32[1,128]{1,0:T(1,128)} %bitcast.12, ...), custom_call_target="tpu_custom_call" | custom-call | tf_op jit(solution)/shard_map/advect_and_solve/pallas_call | solution.py:620
  117.3 5.7 %recover_nodes.1 = f32[3,16,10368]{2,1,0:T(8,128)} custom-call(f32[3,16,81,128]{3,2,1,0:T(8,128)} %get-tuple-element.12.mid_ref, f32[3,64,1024]{2,1,0:T(8,128)} %get-tuple-element.13.mine_ref, f32[3,64,1024]{2,1,0:T(8,128)} %get-tuple-element.14.other_ref, f32[8,128]{1,0:T(8,128)} %get-tuple-element.15.side_ref, f32[8,2048]{1,0:T(8,128)} %get-tuple-element.16.kinds, ...), custom_call_target="tpu_custom_call" | custom-call | tf_op jit(solution)/shard_map/recover_nodes/pallas_call | solution.py:692

commit v2 on v1

--- a/solution.py
+++ b/solution.py
@@ -373,9 +373,17 @@
         core = lax.axis_index("elem")
         barrier = pltpu.get_barrier_semaphore()
 
+        def peer_at(step):
+            bits = count.bit_length() - 1
+            peer = 0
+            for bit in range(bits):
+                weight = count // 2 // 2**bit
+                peer = peer + weight * ((me // weight + step // 2**bit) % 2)
+            return peer
+
         def greet(step, carry):
             pl.semaphore_signal(
-                barrier, inc=1, device_id={"planes": lax.rem(me + step, count)}, device_id_type=pl.DeviceIdType.MESH
+                barrier, inc=1, device_id={"planes": peer_at(step)}, device_id_type=pl.DeviceIdType.MESH
             )
             return carry
 
@@ -404,16 +412,10 @@
 
         def start_all(source, target, way, comp):
             def one(step, carry):
-                copy_to(source, target, way, comp, lax.rem(me + count // 2 + step, count)).start()
+                copy_to(source, target, way, comp, peer_at(step)).start()
                 return carry
 
-            lax.fori_loop(0, count // 2, one, 0)
-
-            def two(step, carry):
-                copy_to(source, target, way, comp, lax.rem(me + step, count)).start()
-                return carry
-
-            lax.fori_loop(1, count // 2, two, 0)
+            lax.fori_loop(1, count, one, 0)
 
         def pair_copy(source, target, at):
             return pltpu.make_async_remote_copy(
@@ -445,13 +447,12 @@
             arrive(comp, me, sent[comp, me])
 
             def one(step, carry):
-                part = lax.rem(me + step, count)
+                part = peer_at(step)
                 copy_from(sent, recv, 0, comp, part).wait_recv()
                 arrive(comp, part, recv[comp, part])
                 return carry
 
-            lax.fori_loop(count // 2, count, one, 0)
-            lax.fori_loop(1, count // 2, one, 0)
+            lax.fori_loop(1, count, one, 0)
 
         def synthesize(comp):
             def one(pair, carry):
@@ -499,7 +500,7 @@
 
         def lift(comp):
             def one(step, carry):
-                copy_from(hats, ret, 1, comp, lax.rem(me + step, count)).wait_recv()
+                copy_from(hats, ret, 1, comp, peer_at(step)).wait_recv()
                 return carry
 
             lax.fori_loop(1, count, one, 0)
@@ -604,7 +605,7 @@
             pair_copy(traces.at[comp], their_traces.at[comp], comps + comp).wait_send()
 
             def drain(step, carry):
-                peer = lax.rem(me + step, count)
+                peer = peer_at(step)
                 copy_to(sent, recv, 0, comp, peer).wait_send()
                 copy_to(hats, ret, 1, comp, peer).wait_send()
                 return carry
@@ -732,7 +733,7 @@
     count = lax.axis_size("planes")
     rows = velocity.shape[1]
     elems = element_kind.shape[0]
-    fits = rows == 16 and elems == LANES and elems * rows == count * LANES and lax.axis_size("elem") == 2
+    fits = count & (count - 1) == 0 and rows == 16 and elems == LANES and elems * rows == count * LANES and lax.axis_size("elem") == 2
     body = fast_device if fits else plain_device
     return body(velocity, geometry, element_kind, *rest)
 

time: 123 us -> 123 us (level)
  no operation moved by 1% of the time
where the time goes in v2:
time: 123 us
  Pallas kernels  123 us (100%)
    pallas_call x1, Pallas kernels, advect_and_solve(): pl.pallas_call(kernel, in_specs=[vmem] * len(operands), out_specs=[vmem]...  117 us
    pallas_call x1, Pallas kernels, recover_nodes(): pl.pallas_call(kernel, grid=(comps,), in_specs=[pl.BlockSpec((1, count, p...  5.73 us

profile of v2, /device:TPU:1, one launch (start us, length us, event | category | flops | bytes accessed | tf_op | source)
XLA Modules:
  0.0 122.9 jit_solution(16501464921252614175)
XLA Ops:
  0.0 117.2 %advect_and_solve.1 = (f32[3,16,81,128]{3,2,1,0:T(8,128)}, f32[3,64,1024]{2,1,0:T(8,128)}, f32[3,64,1024]{2,1,0:T(8,128)}, f32[8,2048]{1,0:T(8,128)}, f32[8,2048...) custom-call(f32[3,16,10368]{2,1,0:T(8,128)} %vel_ref.1, f32[4,10368]{1,0:T(4,128)} %geo_ref.1, s32[1,128]{1,0:T(1,128)} %bitcast.12, ...), custom_call_target="tpu_custom_call" | custom-call | tf_op jit(solution)/shard_map/advect_and_solve/pallas_call | solution.py:621
  117.2 5.7 %recover_nodes.1 = f32[3,16,10368]{2,1,0:T(8,128)} custom-call(f32[3,16,81,128]{3,2,1,0:T(8,128)} %get-tuple-element.12.mid_ref, f32[3,64,1024]{2,1,0:T(8,128)} %get-tuple-element.13.mine_ref, f32[3,64,1024]{2,1,0:T(8,128)} %get-tuple-element.14.other_ref, f32[8,128]{1,0:T(8,128)} %get-tuple-element.15.side_ref, f32[8,2048]{1,0:T(8,128)} %get-tuple-element.16.kinds, ...), custom_call_target="tpu_custom_call" | custom-call | tf_op jit(solution)/shard_map/recover_nodes/pallas_call | solution.py:693

commit v3 on v2

--- a/solution.py
+++ b/solution.py
@@ -364,7 +364,8 @@
     def kernel(
         vel_ref, geo_ref, kind_ref, scale_ref, fixed_ref, stiff_ref, mass_ref, lift_in, recover_in,
         forward_ref, backward_ref, deriv_ref,
-        mid, mine_out, other_out, kinds, factor, recover_out, side_ref,
+        out,
+        mid, mine, kinds, factor, recover_out, side_ref,
         sent, recv, hats, ret, store, fields, slopes, own, away, other, traces, their_traces, facts_out, their_facts,
         geo, lift_ref, mat_ref, lam_ref,
         send_sem, recv_sem, pair_send, pair_recv,
@@ -526,12 +527,35 @@
 
         def solve(comp):
             pair_copy(away.at[comp], other.at[comp], comp).wait_recv()
-            mine, theirs = solve_rows(
+            kept, theirs = solve_rows(
                 own[comp], other[comp], facts_out[...], their_facts[...], lam_ref[0:1], side_ref[0:1], mat_ref[...]
             )
-            mine_out[comp] = mine
+            mine[comp] = kept
             traces[comp] = theirs
             pair_copy(traces.at[comp], their_traces.at[comp], comps + comp).start()
+
+        def recover(comp):
+            pair_copy(traces.at[comp], their_traces.at[comp], comps + comp).wait_recv()
+            second = side_ref[0:1] > 0.5
+            bit = lax.broadcasted_iota(jnp.int32, (4 * SUB, LANES), 1) // 8 % 2 == 0
+            tiles = []
+            for tile in range(half // LANES):
+                at = slice(tile * LANES, (tile + 1) * LANES)
+                first_half = mine[comp, :, at]
+                last_half = their_traces[comp, :, at]
+                low_rows = jnp.where(second, last_half, first_half)
+                high_rows = jnp.where(second, first_half, last_half)
+                tiles.append(jnp.where(bit, low_rows, pltpu.roll(high_rows, 8, 1)))
+                tiles.append(jnp.where(bit, pltpu.roll(low_rows, LANES - 8, 1), high_rows))
+            both = mm(stacked_weights(recover_out[...]), stacked_values(jnp.concatenate(tiles, axis=1)))
+            found = jnp.where(kinds[0:1] > 0.5, both[88 : 88 + points], both[:points])
+            for part in range(count):
+                at = slice(part * LANES, (part + 1) * LANES)
+                block = mid[comp, part] * factor[0:1, at] + found[:, at]
+                block = jnp.concatenate([block, jnp.zeros((LANES - points, LANES), F32)], axis=0).T
+                for local in range(per):
+                    start = (part * per + local) * points
+                    out[comp, :, start : start + points] = block[local * rows : (local + 1) * rows, :points]
 
         def prepare():
             group = iota((4 * SUB, 4 * QUAD), 0)
@@ -595,10 +619,10 @@
         pair_copy(facts_out, their_facts, 2 * comps).wait_recv()
         for comp in range(comps):
             lift(comp)
+            if comp > 0:
+                recover(comp - 1)
             solve(comp)
-        for comp in range(comps):
-            pair_copy(traces.at[comp], their_traces.at[comp], comps + comp).wait_recv()
-            other_out[comp] = their_traces[comp]
+        recover(comps - 1)
         pair_copy(facts_out, their_facts, 2 * comps).wait_send()
         for comp in range(comps):
             pair_copy(away.at[comp], other.at[comp], comp).wait_send()
@@ -621,17 +645,17 @@
     return pl.pallas_call(
         kernel,
         in_specs=[vmem] * len(operands),
-        out_specs=[vmem] * 7,
-        out_shape=[
-            jax.ShapeDtypeStruct(message, F32),
-            jax.ShapeDtypeStruct(piece, F32),
-            jax.ShapeDtypeStruct(piece, F32),
-            jax.ShapeDtypeStruct((8, 2 * half), F32),
-            jax.ShapeDtypeStruct((8, 2 * half), F32),
-            jax.ShapeDtypeStruct((2 * 88, 4 * SUB), F32),
-            jax.ShapeDtypeStruct((8, LANES), F32),
-        ],
-        scratch_shapes=[pltpu.VMEM(message, F32)] * 4
+        out_specs=vmem,
+        out_shape=jax.ShapeDtypeStruct(velocity.shape, F32),
+        scratch_shapes=[
+            pltpu.VMEM(message, F32),
+            pltpu.VMEM(piece, F32),
+            pltpu.VMEM((8, 2 * half), F32),
+            pltpu.VMEM((8, 2 * half), F32),
+            pltpu.VMEM((2 * 88, 4 * SUB), F32),
+            pltpu.VMEM((8, LANES), F32),
+        ]
+        + [pltpu.VMEM(message, F32)] * 4
         + [
             pltpu.VMEM((pairs, planes, 2 * LANES), F32),
             pltpu.VMEM((comps, pairs, 2 * planes, 2 * LANES), F32),
@@ -659,49 +683,6 @@
     )(*operands)
 
 
-def recover_nodes(mid, mine, other, side, kind_lanes, weight_lanes, recover_cols, rows):
-    comps, count, points, _ = mid.shape
-    half = mine.shape[2]
-    per = LANES // rows
-    nodes = count * per * points
-    second_at = recover_cols.shape[0] // 2
-
-    def kernel(mid_ref, mine_ref, other_ref, side_ref, kinds, factor, weights, out):
-        second = side_ref[0:1] > 0.5
-        bit = lax.broadcasted_iota(jnp.int32, (4 * SUB, LANES), 1) // 8 % 2 == 0
-        tiles = []
-        for tile in range(half // LANES):
-            at = slice(tile * LANES, (tile + 1) * LANES)
-            first_half = mine_ref[0, :, at]
-            last_half = other_ref[0, :, at]
-            low_rows = jnp.where(second, last_half, first_half)
-            high_rows = jnp.where(second, first_half, last_half)
-            tiles.append(jnp.where(bit, low_rows, pltpu.roll(high_rows, 8, 1)))
-            tiles.append(jnp.where(bit, pltpu.roll(low_rows, LANES - 8, 1), high_rows))
-        both = mm(stacked_weights(weights[...]), stacked_values(jnp.concatenate(tiles, axis=1)))
-        found = jnp.where(kinds[0:1] > 0.5, both[second_at : second_at + points], both[:points])
-        for part in range(count):
-            at = slice(part * LANES, (part + 1) * LANES)
-            block = mid_ref[0, part] * factor[0:1, at] + found[:, at]
-            block = jnp.concatenate([block, jnp.zeros((LANES - points, LANES), F32)], axis=0).T
-            for local in range(per):
-                start = (part * per + local) * points
-                out[0, :, start : start + points] = block[local * rows : (local + 1) * rows, :points]
-
-    piece = pl.BlockSpec((1, 4 * SUB, half), lambda c: (c, 0, 0))
-    extra = (side, kind_lanes, weight_lanes, recover_cols)
-    return pl.pallas_call(
-        kernel,
-        grid=(comps,),
-        in_specs=[pl.BlockSpec((1, count, points, LANES), lambda c: (c, 0, 0, 0)), piece, piece]
-        + [whole_spec(item.shape) for item in extra],
-        out_specs=pl.BlockSpec((1, rows, nodes), lambda c: (c, 0, 0)),
-        out_shape=jax.ShapeDtypeStruct((comps, rows, nodes), F32),
-        compiler_params=params(),
-        name="recover_nodes",
-    )(mid, mine, other, *extra)
-
-
 def fast_device(
     velocity,
     geometry,
@@ -714,7 +695,7 @@
     recover,
 ):
     count = lax.axis_size("planes")
-    mid, mine, other, kinds, factor, recover_cols, side = advect_and_solve(
+    return advect_and_solve(
         velocity,
         geometry,
         element_kind[None],
@@ -726,7 +707,6 @@
         recover.transpose(2, 0, 1),
         count,
     )
-    return recover_nodes(mid, mine, other, side, kinds, factor, recover_cols, velocity.shape[1])
 
 
 def per_device(velocity, geometry, element_kind, *rest):

time: 123 us -> 121 us (0.984)
  Pallas kernels: 123 us -> 118 us
  local copies, waits for them, and re-layouts: 0 us -> 2.96 us
    pallas_call x2 -> x1, Pallas kernels: 123 us -> 118 us  [advect_and_solve(): pl.pallas_call(kernel, in_specs=[vmem] * len(operands), out_specs=vmem, o...]
    unnamed x0 -> x1, local copies, waits for them, and re-layouts: none -> 2.96 us
where the time goes in v3:
time: 121 us
  Pallas kernels  118 us (98%)
  local copies, waits for them, and re-layouts  2.96 us (2%)
    pallas_call x1, Pallas kernels, advect_and_solve(): pl.pallas_call(kernel, in_specs=[vmem] * len(operands), out_specs=vmem, o...  118 us
    unnamed x1, local copies, waits for them, and re-layouts  2.96 us

profile of v3, /device:TPU:1, one launch (start us, length us, event | category | flops | bytes accessed | tf_op | source)
XLA Modules:
  0.0 120.6 jit_solution(6345089931333576295)
XLA Ops:
  0.0 117.6 %advect_and_solve.1 = f32[3,16,10368]{2,1,0:T(8,128)} custom-call(f32[3,16,10368]{2,1,0:T(8,128)} %vel_ref.1, f32[4,10368]{1,0:T(4,128)} %geo_ref.1, s32[1,128]{1,0:T(1,128)} %bitcast.12, f32[1,128]{1,0:T(1,128)} %bitcast.13, s32[9,2,128]{2,1,0:T(2,128)} %bitcast.11, f32[36,2,36]{2,1,0:T(2,128)} %bitcast.7, f32[36,2,36]{2,1,0:T(2,128)} %bitcast.8, ...), custom_call_target="tpu_custom_call" | custom-call | tf_op jit(solution)/shard_map/advect_and_solve/pallas_call | solution.py:645
  117.6 3.0 %copy.14 = f32[3,16,10368]{2,1,0:T(8,128)} copy(f32[3,16,10368]{2,1,0:T(8,128)} %advect_and_solve.1) | data formatting | bytes 3981312
